TPU v7x, 256 devices: a whole 4x4x8 slice. The times are simulated.
256 devices in a mesh: ctx: 16 (over y, x), exp: 8 (over z), dp: 2 (over core).
Axes of the slice: x: 4, y: 4, z: 8, core: 2. Of those that a mesh axis runs over, the one named last changes fastest.
Arguments:
- residual: bfloat16 [2048, 4096], P('ctx', ('exp', 'dp')), may hold values from -6 to 6
- ssm_values: bfloat16 [2048, 4096], P('ctx', ('exp', 'dp')), may hold values from -6 to 6
- ssm_keys: bfloat16 [2048, 64], P('ctx'), may hold values from -6 to 6
- ssm_queries: bfloat16 [2048, 64], P('ctx'), may hold values from -0.015625 to 0.015625
- log_decay: float32 [2048, 64], P('ctx', ('exp', 'dp')), may hold values from -1 to 0, as said below
- expert_ids: int32 [2048, 2], P('ctx'), may hold values from 0 to 7, all different within a row; in each aligned block of 128 rows (0 to 127, 128 to 255, ...) at most 40 rows name the same one
- gate_probs: float32 [2048, 2], P('ctx'), may hold values from 0.2 to 1
- norm_gain: float32 [4096], P(('exp', 'dp')), may hold values from 0.5 to 1.5
- w_gate: bfloat16 [8, 4096, 8192], P('exp', None, ('ctx', 'dp')), may hold values from -0.09375 to 0.09375
- w_up: bfloat16 [8, 4096, 8192], P('exp', None, ('ctx', 'dp')), may hold values from -0.09375 to 0.09375
- w_down: bfloat16 [8, 4096, 8192], P('exp', None, ('ctx', 'dp')), may hold values from -0.0625 to 0.0625
- out_grad: bfloat16 [2048, 4096], P('ctx', ('exp', 'dp')), may hold values from -6 to 6
Outputs:
- grad_residual: bfloat16 [2048, 4096], P('ctx', ('exp', 'dp'))
- grad_values: bfloat16 [2048, 4096], P('ctx', ('exp', 'dp'))
- grad_keys: float32 [2048, 64], P('ctx')
- grad_queries: float32 [2048, 64], P('ctx')
- grad_decay: float32 [2048, 64], P('ctx', ('exp', 'dp'))
- grad_probs: float32 [2048, 2], P('ctx')
- grad_gain: float32 [4096], P(('exp', 'dp'))
- w_gate_grad: bfloat16 [8, 4096, 8192], P('exp', None, ('ctx', 'dp'))
- w_up_grad: bfloat16 [8, 4096, 8192], P('exp', None, ('ctx', 'dp'))
- w_down_grad: bfloat16 [8, 4096, 8192], P('exp', None, ('ctx', 'dp'))
Inputs may be any that keep to these rules, and one draw needn't show every extreme that they name: `expert_ids`: each token names two different experts; among the 128 tokens of one index of ctx (aligned blocks) no expert is named more than 40 times, a bound that some block reaches. `log_decay`: negative everywhere.
All inputs are finite; a program needn't handle non-finite values.
Results may differ from a plain program's by a relative error of at most 0.028.
Values may be sent and summed in bfloat16 or wider, within the bound.
No kernel may reach another device: no remote copies, remote signals or barrier semaphores. Data moves between devices by JAX's collectives and lax.ppermute only.
A program may use at most 128 MiB of HBM per device.

v0:
```python
import jax
import jax.numpy as jnp
from jax import lax
from jax.sharding import PartitionSpec as P

HIGH = lax.Precision.HIGHEST
EPS = 1e-05


def entering(x, axis, join, neutral):
    place = lax.axis_index(axis)
    gathered = jax.tree.map(
        lambda a, kind: lax.all_gather(a.astype(kind), axis), x, (jnp.bfloat16, jnp.bfloat16)
    )
    state = jax.tree.map(lambda a, e: jnp.zeros_like(a) + jnp.asarray(e, a.dtype), x, neutral)

    def entering_one(step, state):
        return join(
            state,
            jax.tree.map(
                lambda a, own: lax.dynamic_index_in_dim(a, step, 0, False).astype(own.dtype),
                gathered,
                x,
            ),
        )

    return lax.fori_loop(0, place, entering_one, state)


def carried_in(x, axis, join, neutral):
    count = lax.axis_size(axis)
    place = lax.axis_index(axis)
    ahead = count - 1 - place
    gathered = jax.tree.map(
        lambda a, kind: lax.all_gather(a.astype(kind), axis),
        x,
        jax.tree.map(lambda a: jnp.bfloat16 if a.dtype == jnp.float32 else a.dtype, x),
    )
    state = jax.tree.map(lambda a, e: jnp.zeros_like(a) + jnp.asarray(e, a.dtype), x, neutral)

    def carried_one(step, state):
        source = count - 1 - step
        return join(
            state,
            jax.tree.map(
                lambda a, own: lax.dynamic_index_in_dim(a, source, 0, False).astype(own.dtype),
                gathered,
                x,
            ),
        )

    return lax.fori_loop(0, ahead, carried_one, state)


def block_state(values, key_rows, log_decay):
    cumulative = jnp.cumsum(log_decay, axis=0)
    total_log = cumulative[-1]
    tail_decay = jnp.exp(total_log[None, :] - cumulative)
    weighted = tail_decay[:, :, None] * values
    state_local = jnp.einsum("shp,sn->hpn", weighted, key_rows, precision=HIGH)
    return (jnp.exp(total_log), state_local)


def block_output(values, key_rows, queries, log_decay, state_in):
    cumulative = jnp.cumsum(log_decay, axis=0)
    length = values.shape[0]
    row_index = lax.broadcasted_iota(jnp.int32, (length, length), 0)
    col_index = lax.broadcasted_iota(jnp.int32, (length, length), 1)
    causal = (row_index >= col_index)[None]
    cum_heads = cumulative.T
    log_gap = jnp.where(causal, cum_heads[:, :, None] - cum_heads[:, None, :], 0.0)
    decay_mat = jnp.where(causal, jnp.exp(log_gap), 0.0)
    scores = jnp.dot(queries, key_rows.T, precision=HIGH)
    inner_part = jnp.einsum("hts,shp->thp", decay_mat * scores[None], values, precision=HIGH)
    carried = jnp.einsum("tn,hpn->thp", queries, state_in, precision=HIGH)
    return inner_part + jnp.exp(cumulative)[:, :, None] * carried


def silu_parts(gate_act):
    sigmoid_val = jax.nn.sigmoid(gate_act)
    return (gate_act * sigmoid_val, sigmoid_val * (1.0 + gate_act * (1.0 - sigmoid_val)))


def route_slots(token_ids, expert_count):
    owners = token_ids.reshape(-1)
    onehot = (owners[:, None] == jnp.arange(expert_count, dtype=jnp.int32)[None, :]).astype(
        jnp.int32
    )
    rank_before = jnp.cumsum(onehot, axis=0) - onehot
    return (owners, jnp.sum(rank_before * onehot, axis=1))


def combine_states(earlier_part, later_part):
    return (
        earlier_part[0] * later_part[0],
        later_part[0][:, None, None] * earlier_part[1] + later_part[1],
    )


def arrange_rows(gathered, ctx_count, dp_count):
    capacity = gathered.shape[1]
    exp_count = gathered.shape[2]
    feat = gathered.shape[3]
    shaped = gathered.reshape(ctx_count, dp_count, capacity, exp_count, feat)
    return shaped.transpose(0, 2, 3, 1, 4).reshape(
        ctx_count * capacity, exp_count * dp_count * feat
    )


def arrange_sums(full_term, ctx_count, dp_count, exp_count, capacity):
    feat = full_term.shape[1] // (exp_count * dp_count)
    shaped = full_term.reshape(ctx_count, capacity, exp_count, dp_count, feat)
    return shaped.transpose(0, 3, 1, 2, 4).reshape(
        ctx_count * dp_count * capacity, exp_count * feat
    )


def per_device(
    residual,
    ssm_values,
    ssm_keys,
    ssm_queries,
    log_decay,
    expert_ids,
    gate_probs,
    norm_gain,
    w_gate,
    w_up,
    w_down,
    out_grad,
):
    tokens = residual.shape[0]
    feat = residual.shape[1]
    heads_here = log_decay.shape[1]
    head_size = feat // heads_here
    model_width = w_gate.shape[1]
    ctx_count = lax.axis_size("ctx")
    exp_count = lax.axis_size("exp")
    dp_count = lax.axis_size("dp")
    expert_count = w_gate.shape[0] * exp_count
    capacity = 5 * tokens // (2 * expert_count)
    block_vals = ssm_values.astype(jnp.float32).reshape(tokens, heads_here, head_size)
    block_keys = ssm_keys.astype(jnp.float32)
    block_queries = ssm_queries.astype(jnp.float32)
    (decay_total, state_local), state_pull = jax.vjp(block_state, block_vals, block_keys, log_decay)
    neutral = (jnp.ones_like(decay_total), jnp.zeros_like(state_local))
    state_in = entering((decay_total, state_local), "ctx", combine_states, neutral)[1]
    mixer_out, output_pull = jax.vjp(
        block_output, block_vals, block_keys, block_queries, log_decay, state_in
    )
    hidden = (residual.astype(jnp.float32) + mixer_out.reshape(tokens, feat)).astype(jnp.bfloat16)
    hidden_f = hidden.astype(jnp.float32)
    square_sum = lax.psum(jnp.sum(hidden_f * hidden_f, axis=1), ("exp", "dp"))
    inv_rms = lax.rsqrt(square_sum / model_width + EPS)[:, None]
    normed = (hidden_f * inv_rms * norm_gain[None, :]).astype(jnp.bfloat16)
    owners, slot_index = route_slots(expert_ids, expert_count)
    pair_rows = jnp.repeat(normed, 2, axis=0)
    dout_rows = jnp.repeat(out_grad, 2, axis=0)
    pair_prob = gate_probs.reshape(-1)
    pair_cot = (pair_prob[:, None] * dout_rows.astype(jnp.float32)).astype(jnp.bfloat16)
    empty = jnp.zeros((expert_count, capacity, feat), jnp.bfloat16)
    send_rows = empty.at[owners, slot_index].set(pair_rows).reshape(expert_count, capacity, 1, feat)
    got_rows = lax.all_to_all(send_rows, "exp", split_axis=0, concat_axis=2, tiled=True)
    all_rows = lax.all_gather(got_rows, ("ctx", "dp"), axis=0, tiled=True)
    rows_flat = arrange_rows(all_rows, ctx_count, dp_count)
    act_gate = jnp.dot(rows_flat, w_gate[0], preferred_element_type=jnp.float32)
    act_up = jnp.dot(rows_flat, w_up[0], preferred_element_type=jnp.float32)
    swish_val, swish_slope = silu_parts(act_gate)
    hidden_act = (swish_val * act_up).astype(jnp.bfloat16)
    full_out = lax.dot_general(
        hidden_act, w_down[0], (((1,), (1,)), ((), ())), preferred_element_type=jnp.float32
    )
    out_total = lax.psum_scatter(
        arrange_sums(full_out, ctx_count, dp_count, exp_count, capacity).astype(jnp.bfloat16),
        ("ctx", "dp"),
        scatter_dimension=0,
        tiled=True,
    )
    expert_out = out_total.reshape(1, capacity, exp_count, feat)
    back_out = lax.all_to_all(expert_out, "exp", split_axis=2, concat_axis=0, tiled=True).reshape(
        expert_count, capacity, feat
    )
    out_pairs = back_out[owners, slot_index]
    probs_part = jnp.einsum(
        "kd,kd->k", out_pairs, dout_rows, preferred_element_type=jnp.float32
    ).reshape(tokens, 2)
    grad_probs = lax.psum(probs_part, ("exp", "dp"))
    send_cot = empty.at[owners, slot_index].set(pair_cot).reshape(expert_count, capacity, 1, feat)
    got_cot = lax.all_to_all(send_cot, "exp", split_axis=0, concat_axis=2, tiled=True)
    all_cot = lax.all_gather(got_cot, ("ctx", "dp"), axis=0, tiled=True)
    cot_flat = arrange_rows(all_cot, ctx_count, dp_count)
    grad_act = jnp.dot(cot_flat, w_down[0], preferred_element_type=jnp.float32)
    grad_gate = (grad_act * act_up * swish_slope).astype(jnp.bfloat16)
    grad_up = (grad_act * swish_val).astype(jnp.bfloat16)
    full_back = lax.dot_general(
        grad_gate, w_gate[0], (((1,), (1,)), ((), ())), preferred_element_type=jnp.float32
    ) + lax.dot_general(
        grad_up, w_up[0], (((1,), (1,)), ((), ())), preferred_element_type=jnp.float32
    )
    back_total = lax.psum_scatter(
        arrange_sums(full_back, ctx_count, dp_count, exp_count, capacity).astype(jnp.bfloat16),
        ("ctx", "dp"),
        scatter_dimension=0,
        tiled=True,
    )
    pair_back = back_total.reshape(1, capacity, exp_count, feat)
    back_in = lax.all_to_all(pair_back, "exp", split_axis=2, concat_axis=0, tiled=True).reshape(
        expert_count, capacity, feat
    )
    grad_normed = (
        back_in[owners, slot_index].astype(jnp.float32).reshape(tokens, 2, feat).sum(axis=1)
    )
    w_gate_grad = jnp.dot(rows_flat.T, grad_gate, preferred_element_type=jnp.float32).astype(
        jnp.bfloat16
    )[None]
    w_up_grad = jnp.dot(rows_flat.T, grad_up, preferred_element_type=jnp.float32).astype(
        jnp.bfloat16
    )[None]
    w_down_grad = jnp.dot(cot_flat.T, hidden_act, preferred_element_type=jnp.float32).astype(
        jnp.bfloat16
    )[None]
    scaled = grad_normed * norm_gain[None, :]
    inner_sum = lax.psum(jnp.sum(hidden_f * scaled, axis=1), ("exp", "dp"))
    projection = (inner_sum / model_width)[:, None]
    grad_hidden = (
        out_grad.astype(jnp.float32) + inv_rms * scaled - hidden_f * inv_rms**3 * projection
    )
    gain_part = jnp.sum(grad_normed * hidden_f * inv_rms, axis=0)
    grad_gain = lax.psum(gain_part, "ctx")
    grad_mixer = grad_hidden.reshape(tokens, heads_here, head_size)
    vals_first, keys_first, queries_part, decay_first, carry_cot = output_pull(grad_mixer)
    grad_state = carried_in((decay_total, carry_cot), "ctx", combine_states, neutral)[1]
    grad_total = jnp.sum(grad_state * state_in, axis=(1, 2))
    vals_second, keys_second, decay_second = state_pull((grad_total, grad_state))
    grad_keys, grad_queries = (
        lax.psum((keys_first + keys_second).astype(jnp.bfloat16), ("exp", "dp")).astype(
            jnp.float32
        ),
        lax.psum(queries_part.astype(jnp.bfloat16), ("exp", "dp")).astype(jnp.float32),
    )
    grad_residual = grad_hidden.astype(jnp.bfloat16)
    grad_values = (vals_first + vals_second).reshape(tokens, feat).astype(jnp.bfloat16)
    grad_decay = decay_first + decay_second
    return (
        grad_residual,
        grad_values,
        grad_keys,
        grad_queries,
        grad_decay,
        grad_probs,
        grad_gain,
        w_gate_grad,
        w_up_grad,
        w_down_grad,
    )


def solution(mesh):
    return jax.shard_map(
        per_device,
        mesh=mesh,
        in_specs=(
            P("ctx", ("exp", "dp")),
            P("ctx", ("exp", "dp")),
            P("ctx", None),
            P("ctx", None),
            P("ctx", ("exp", "dp")),
            P("ctx", None),
            P("ctx", None),
            P(("exp", "dp")),
            P("exp", None, ("ctx", "dp")),
            P("exp", None, ("ctx", "dp")),
            P("exp", None, ("ctx", "dp")),
            P("ctx", ("exp", "dp")),
        ),
        out_specs=(
            P("ctx", ("exp", "dp")),
            P("ctx", ("exp", "dp")),
            P("ctx", None),
            P("ctx", None),
            P("ctx", ("exp", "dp")),
            P("ctx", None),
            P(("exp", "dp")),
            P("exp", None, ("ctx", "dp")),
            P("exp", None, ("ctx", "dp")),
            P("exp", None, ("ctx", "dp")),
        ),
        check_vma=False,
    )
```

profile of v0, /device:TPU:2, one launch (start us, length us, event | category | flops | bytes accessed | tf_op | source)
XLA Modules:
  0.0 650.5 jit_solution(5369685150378966095)
XLA Ops:
  7.3 0.9 copy.158
  9.5 0.8 copy.161
  10.4 0.9 broadcast_in_dim.74
  11.6 13.2 %scatter_fusion = bf16[8,40,256]{2,1,0:T(8,128)(2,1)S(1)} fusion(bf16[8,40,256]{2,1,0:T(8,128)(2,1)S(1)} %broadcast_in_dim.73.clone.1, s32[256]{0:T(256)S(1)} %bitcast.193, bf16[256,256]{1,0:T(8,128)(2,1)S(1)} %fusion.19), kind=kCustom, calls=%fused_computation.2 | custom fusion | bytes 395264 | tf_op jit(solution)/shard_map/scatter | solution.py:188
  24.9 18.0 %all_to_all.66 = bf16[8,40,1,256]{3,1,2,0:T(8,128)(2,1)S(1)} all-to-all(bf16[8,40,1,256]{3,1,2,0:T(8,128)(2,1)S(1)} %bitcast.200), channel_id=1, replica_groups=mesh['ctx'=16,'exp'=8,'dp'=2] {'exp'}, dimensions={0} | all-to-all | bytes 327680 | tf_op jit(solution)/shard_map/all_to_all | solution.py:189
  44.6 20.7 %all-gather.4 = bf16[16,1,4]{2,1,0:T(2,128)(2,1)S(1)} all-gather(bf16[1,1,4]{2,1,0:T(2,128)(2,1)S(1)} %get-tuple-element.299), channel_id=1, replica_groups=mesh['ctx'=16,'exp'=8,'dp'=2] {'ctx'}, dimensions={0}, use_global_device_ids=true | all-gather | bytes 136 | tf_op jit(solution)/shard_map/all_gather | solution.py:13
  65.4 1.0 copy.152
  67.0 27.6 %all-gather = bf16[64,64,64]{2,1,0:T(8,128)(2,1)} all-gather(bf16[4,64,64]{2,1,0:T(8,128)(2,1)S(1)} %convolution_convert_fusion.4), channel_id=2, replica_groups=mesh['ctx'=16,'exp'=8,'dp'=2] {'ctx'}, dimensions={0}, use_global_device_ids=true | all-gather | bytes 557056 | tf_op jit(solution)/shard_map/all_gather | solution.py:13
  94.8 1.0 while.26
  94.9 0.9 convert_add_fusion.4
  96.7 23.5 %psum.42 = f32[128]{0:T(128)S(1)} all-reduce(f32[128]{0:T(128)S(1)} %get-tuple-element.291), channel_id=1, replica_groups=mesh['ctx'=16,'exp'=8,'dp'=2] {'exp','dp'}, use_global_device_ids=true, to_apply=%region_4.5 | all-reduce | flops 128 | bytes 1024 | tf_op jit(solution)/shard_map/psum | solution.py:153
  121.1 13.2 %scatter_fusion.1 = bf16[8,40,256]{2,1,0:T(8,128)(2,1)S(1)} fusion(bf16[8,40,256]{2,1,0:T(8,128)(2,1)S(1)} %broadcast_in_dim.73.clone, s32[256]{0:T(256)S(1)} %bitcast.194, bf16[256,256]{1,0:T(8,128)(2,1)S(1)} %reshape.273), kind=kCustom, calls=%fused_computation.3 | custom fusion | bytes 395264 | tf_op jit(solution)/shard_map/scatter | solution.py:162
  134.3 12.5 %all_to_all.67 = bf16[8,40,1,256]{3,1,2,0:T(8,128)(2,1)S(1)} all-to-all(bf16[8,40,1,256]{3,1,2,0:T(8,128)(2,1)S(1)} %bitcast.199), channel_id=1, replica_groups=mesh['ctx'=16,'exp'=8,'dp'=2] {'exp'}, dimensions={0} | all-to-all | bytes 327680 | tf_op jit(solution)/shard_map/all_to_all | solution.py:163
  148.1 13.0 %copy.164 = bf16[16,40,8,2,256]{4,3,2,1,0:T(2,128)(2,1)} copy(bf16[16,40,8,2,256]{4,2,1,3,0:T(8,128)(2,1)} %bitcast.203) | data formatting | bytes 10485760 | tf_op jit(solution)/shard_map/transpose | solution.py:105
  161.1 9.6 %reshape.236 = bf16[640,4096]{1,0:T(8,128)(2,1)} reshape(bf16[16,40,8,2,256]{4,3,2,1,0:T(2,128)(2,1)} %copy.164) | data formatting | bytes 10485760 | tf_op jit(solution)/shard_map/reshape | solution.py:105
  170.7 35.8 %all-gather.10.cloned.1.call-done = bf16[32,40,8,1,256]{4,2,3,1,0:T(8,128)(2,1)} async-done(((bf16[1,40,8,1,256]{4,2,3,1,0:T(8,128)(2,1)}), bf16[32,40,8,1,256]{4,2,3,1,0:T(8,128)(2,1)}) %all-gather.10.cloned.1.call-update) | async-done | bytes 5242896 | tf_op jit(solution)/shard_map/all_gather | solution.py:164
  206.6 13.0 %copy.167 = bf16[16,40,8,2,256]{4,3,2,1,0:T(2,128)(2,1)} copy(bf16[16,40,8,2,256]{4,2,1,3,0:T(8,128)(2,1)} %bitcast.204) | data formatting | bytes 10485760 | tf_op jit(solution)/shard_map/transpose | solution.py:105
  219.6 9.6 %reshape.240 = bf16[640,4096]{1,0:T(8,128)(2,1)} reshape(bf16[16,40,8,2,256]{4,3,2,1,0:T(2,128)(2,1)} %copy.167) | data formatting | bytes 10485760 | tf_op jit(solution)/shard_map/reshape | solution.py:105
  229.2 4.2 fusion.10
  233.9 1.5 fusion.5
  235.5 2.4 multiply_convert_fusion
  238.0 1.6 convert_bitcast_fusion
  239.6 2.3 copy.176
  241.9 4.6 copy.191
  247.0 1.1 copy-done.4
  248.2 1.6 fusion.3
  249.8 3.8 add_convert_fusion
  253.6 9.6 %convert_element_type.165 = bf16[16,40,8,2,256]{4,3,2,1,0:T(2,128)(2,1)} reshape(bf16[640,4096]{1,0:T(8,128)(2,1)} %add_convert_fusion) | data formatting | bytes 10485760 | tf_op jit(solution)/shard_map/convert_element_type | solution.py:201
  263.2 3.6 copy.168
  266.8 4.5 copy.189
  271.3 1.0 copy-done.10
  272.3 5.9 fusion.2
  278.2 60.3 %reduce-scatter.5.cloned.1.call-done = bf16[40,2048]{1,0:T(8,128)(2,1)} async-done(((bf16[1280,2048]{1,0:T(8,128)(2,1)}), bf16[40,2048]{1,0:T(8,128)(2,1)}) %reduce-scatter.5.cloned.1.call-update) | async-done | bytes 163856 | tf_op jit(solution)/shard_map/reduce_scatter | solution.py:173
  338.5 0.9 copy.192
  340.1 7.0 %all-to-all-start.3 = ((bf16[1,40,8,256]{3,1,0,2:T(8,128)(2,1)}), bf16[1,40,8,256]{3,1,0,2:T(8,128)(2,1)S(1)}, u32[]{:S(2)}, u32[]{:S(2)}) async-start(bf16[1,40,8,256]{3,1,0,2:T(8,128)(2,1)} %copy.177), calls=%async_computation.5 | async-start | bytes 327680 | tf_op jit(solution)/shard_map/all_to_all | solution.py:180
  347.2 5.7 fusion
  352.9 81.2 %reduce-scatter.3.cloned.1.call-done = bf16[40,2048]{1,0:T(8,128)(2,1)} async-done(((bf16[1280,2048]{1,0:T(8,128)(2,1)}), bf16[40,2048]{1,0:T(8,128)(2,1)}) %reduce-scatter.3.cloned.1.call-update) | async-done | bytes 163856 | tf_op jit(solution)/shard_map/reduce_scatter | solution.py:200
  434.1 0.9 copy.190
  435.8 7.2 %all-to-all-start.2 = ((bf16[1,40,8,256]{3,1,0,2:T(8,128)(2,1)}), bf16[1,40,8,256]{3,1,0,2:T(8,128)(2,1)S(1)}, u32[]{:S(2)}, u32[]{:S(2)}) async-start(bf16[1,40,8,256]{3,1,0,2:T(8,128)(2,1)} %copy.169), calls=%async_computation.3 | async-start | bytes 327680 | tf_op jit(solution)/shard_map/all_to_all | solution.py:207
  443.0 5.7 fusion.1
  448.7 1.7 gather_fusion.1
  450.6 1.7 all-to-all-done.2
  452.4 1.7 gather_fusion
  454.6 46.5 %all-reduce.1 = (f32[128]{0:T(128)S(1)}, f32[128,2]{1,0:T(8,128)S(1)}) all-reduce(f32[128]{0:T(128)S(1)} %get-tuple-element.264, f32[128,2]{1,0:T(8,128)S(1)} %reshape.247), channel_id=1, replica_groups=mesh['ctx'=16,'exp'=8,'dp'=2] {'exp','dp'}, use_global_device_ids=true, to_apply=%region_13.14 | all-reduce | flops 384 | bytes 3072 | tf_op jit(solution)/shard_map/psum | solution.py:223
  502.6 25.1 %all-gather.3 = bf16[64,64,64]{2,1,0:T(8,128)(2,1)} all-gather(bf16[4,64,64]{2,1,0:T(8,128)(2,1)S(1)} %convolution_convert_fusion.3), channel_id=5, replica_groups=mesh['ctx'=16,'exp'=8,'dp'=2] {'ctx'}, dimensions={0}, use_global_device_ids=true | all-gather | bytes 557056 | tf_op jit(solution)/shard_map/all_gather | solution.py:35
  527.7 22.9 %while.27 = (s32[]{:T(128)}, f32[4,64,64]{2,1,0:T(8,128)S(1)}, s32[]{:T(128)}, bf16[16,4]{1,0:T(8,128)(2,1)}, bf16[16,4,64,64]{3,2,1,0:T(8,128)(2,1)}, /*index=5*/s32[]{:T(128)}, s32[]{:T(128)}, s32[]{:T(128)}, s32[]{:T(128)}) while((s32[]{:T(128)}, f32[4,64,64]{2,1,0:T(8,128)S(1)}, s32[]{:T(128)}, bf16[16,4]{1,0:T(8,128)(2,1)}, ...), condition=%wide.region_15.16_spmd, body=%wide.region_14.15_spmd.sunk | while | flops 49162 | bytes 164035 | solution.py:52
  528.4 0.9 convert_add_fusion.5
  530.0 0.9 convert_add_fusion.5
  531.7 0.9 convert_add_fusion.5
  533.3 0.9 convert_add_fusion.5
  534.9 0.9 convert_add_fusion.5
  536.6 0.9 convert_add_fusion.5
  538.2 0.9 convert_add_fusion.5
  539.8 0.9 convert_add_fusion.5
  541.5 0.9 convert_add_fusion.5
  543.1 0.9 convert_add_fusion.5
  544.8 0.9 convert_add_fusion.5
  546.4 0.9 convert_add_fusion.5
  548.0 0.9 convert_add_fusion.5
  549.7 0.9 convert_add_fusion.5
  550.9 39.5 %psum.47 = f32[256]{0:T(256)} all-reduce(f32[256]{0:T(256)S(1)} %get-tuple-element.263), channel_id=1, replica_groups=mesh['ctx'=16,'exp'=8,'dp'=2] {'ctx'}, use_global_device_ids=true, to_apply=%region_30.31 | all-reduce | flops 256 | bytes 2048 | tf_op jit(solution)/shard_map/psum | solution.py:229
  593.7 45.7 %all-reduce.2 = (bf16[128,64]{0,1:T(8,128)(2,1)S(1)}, bf16[128,64]{0,1:T(8,128)(2,1)S(1)}) all-reduce(bf16[128,64]{0,1:T(8,128)(2,1)S(1)} %fusion.16, bf16[128,64]{0,1:T(8,128)(2,1)S(1)} %fusion.17), channel_id=1, replica_groups=mesh['ctx'=16,'exp'=8,'dp'=2] {'exp','dp'}, use_global_device_ids=true, to_apply=%region_17.18 | all-reduce | flops 16384 | bytes 65536 | tf_op jit(solution)/shard_map/psum | solution.py:236
  640.8 1.1 reduce_window_sum.47
  641.9 1.1 reduce_window_sum.48
  (139 shorter events, 27.4 us)
Async XLA Ops:
  7.2 222.0 %copy-start = (bf16[1,4096,256]{2,1,0:T(8,128)(2,1)S(1)}, bf16[1,4096,256]{2,1,0:T(8,128)(2,1)}, u32[]{:S(2)}) copy-start(bf16[1,4096,256]{2,1,0:T(8,128)(2,1)} %param.26) | copy-start | bytes 6291460
  7.2 59.6 %copy-start.13 = (bf16[128,64]{0,1:T(8,128)(2,1)S(1)}, bf16[128,64]{0,1:T(8,128)(2,1)}, u32[]{:S(2)}) copy-start(bf16[128,64]{0,1:T(8,128)(2,1)} %param.18) | copy-start | bytes 49156
  7.2 87.4 %copy-start.12 = (bf16[128,64]{0,1:T(8,128)(2,1)S(1)}, bf16[128,64]{0,1:T(8,128)(2,1)}, u32[]{:S(2)}) copy-start(bf16[128,64]{0,1:T(8,128)(2,1)} %param.19) | copy-start | bytes 49156
  7.2 89.4 %copy-start.16 = (bf16[128,256]{1,0:T(8,128)(2,1)S(1)}, bf16[128,256]{1,0:T(8,128)(2,1)}, u32[]{:S(2)}) copy-start(bf16[128,256]{1,0:T(8,128)(2,1)} %param.16) | copy-start | bytes 196612
  7.2 113.6 %copy-start.17 = (f32[256]{0:T(256)S(1)}, f32[256]{0:T(256)}, u32[]{:S(2)}) copy-start(f32[256]{0:T(256)} %param.23) | copy-start | bytes 3076
  7.2 140.9 %all-gather.8.cloned.1.call-start = ((), (), s32[]{:S(2)}) async-start(), calls=%async_computation.8 | async-start | bytes 5406720 | tf_op jit(solution)/shard_map/all_gather | solution.py:190
  43.6 163.0 %all-gather.10.cloned.1.call-start = ((), (), s32[]{:S(2)}) async-start(), calls=%async_computation.9 | async-start | bytes 5406720 | tf_op jit(solution)/shard_map/all_gather | solution.py:164
  66.4 67.9 %copy-start.19 = (f32[4,128]{1,0:T(4,128)}, f32[4,128]{1,0:T(4,128)S(1)}, u32[]{:S(2)}) copy-start(f32[4,128]{1,0:T(4,128)S(1)} %copy.150) | copy-start | bytes 6148
  94.8 39.5 %copy-start.14 = (f32[128,128]{1,0:T(8,128)}, f32[128,128]{1,0:T(8,128)S(1)}, u32[]{:S(2)}) copy-start(f32[128,128]{1,0:T(8,128)S(1)} %fusion.65) | copy-start | bytes 196612
  95.8 38.5 %copy-start.18 = (bf16[16,4]{1,0:T(8,128)(2,1)}, bf16[16,4]{1,0:T(8,128)(2,1)S(1)}, u32[]{:S(2)}) copy-start(bf16[16,4]{1,0:T(8,128)(2,1)S(1)} %get-tuple-element.437) | copy-start | bytes 388
  147.5 191.0 %reduce-scatter.5.cloned.1.call-start = ((), (), s32[]{:S(2)}) async-start(), calls=%async_computation.7 | async-start | bytes 5406720 | tf_op jit(solution)/shard_map/reduce_scatter | solution.py:173
  229.2 4.2 copy-start.2
  229.2 4.7 copy-start.3
  233.9 1.6 copy-start.5
  238.0 3.9 copy-start.9
  246.6 1.6 copy-start.4
  246.6 187.5 %reduce-scatter.3.cloned.1.call-start = ((), (), s32[]{:S(2)}) async-start(), calls=%async_computation.6 | async-start | bytes 5406720 | tf_op jit(solution)/shard_map/reduce_scatter | solution.py:200
  248.2 1.6 copy-start.6
  248.2 1.6 copy-start.7
  271.3 1.0 copy-start.10
  340.1 95.7 %all-to-all-start.3 = ((bf16[1,40,8,256]{3,1,0,2:T(8,128)(2,1)}), bf16[1,40,8,256]{3,1,0,2:T(8,128)(2,1)S(1)}, u32[]{:S(2)}, u32[]{:S(2)}) async-start(bf16[1,40,8,256]{3,1,0,2:T(8,128)(2,1)} %copy.177), calls=%async_computation.5 | async-start | bytes 327680 | tf_op jit(solution)/shard_map/all_to_all | solution.py:180
  347.2 95.8 %copy-start.8 = (bf16[640,256]{1,0:T(8,128)(2,1)S(1)}, bf16[640,256]{1,0:T(8,128)(2,1)}, u32[]{:S(2)}) copy-start(bf16[640,256]{1,0:T(8,128)(2,1)} %get-tuple-element.297) | copy-start | bytes 983044
  435.8 16.6 %all-to-all-start.2 = ((bf16[1,40,8,256]{3,1,0,2:T(8,128)(2,1)}), bf16[1,40,8,256]{3,1,0,2:T(8,128)(2,1)S(1)}, u32[]{:S(2)}, u32[]{:S(2)}) async-start(bf16[1,40,8,256]{3,1,0,2:T(8,128)(2,1)} %copy.169), calls=%async_computation.3 | async-start | bytes 327680 | tf_op jit(solution)/shard_map/all_to_all | solution.py:207
  443.0 58.1 %copy-start.11 = (bf16[128,256]{1,0:T(8,128)(2,1)S(1)}, bf16[128,256]{1,0:T(8,128)(2,1)}, u32[]{:S(2)}) copy-start(bf16[128,256]{1,0:T(8,128)(2,1)} %param.27) | copy-start | bytes 196612
  443.0 58.1 %copy-start.21 = (f32[128]{0:T(128)S(1)}, f32[128]{0:T(128)}, u32[]{:S(2)}) copy-start(f32[128]{0:T(128)} %get-tuple-element.300) | copy-start | bytes 1540
  448.7 142.3 %copy-start.15 = (f32[128,128]{1,0:T(8,128)S(1)}, f32[128,128]{1,0:T(8,128)}, u32[]{:S(2)}) copy-start(f32[128,128]{1,0:T(8,128)} %copy-done.14) | copy-start | bytes 196612
  448.7 142.3 %copy-start.20 = (f32[4,128]{1,0:T(4,128)S(1)}, f32[4,128]{1,0:T(4,128)}, u32[]{:S(2)}) copy-start(f32[4,128]{1,0:T(4,128)} %copy-done.19) | copy-start | bytes 6148
  452.4 191.4 %copy-start.1 = (bf16[1,4096,256]{2,1,0:T(8,128)(2,1)S(1)}, bf16[1,4096,256]{2,1,0:T(8,128)(2,1)}, u32[]{:S(2)}) copy-start(bf16[1,4096,256]{2,1,0:T(8,128)(2,1)} %param.26) | copy-start | bytes 6291460
Sparse Core Ops, SparseCore 0:
  43.7 49.1 all-gather.7
  147.6 58.8 all-gather.9
  246.7 91.7 reduce-scatter.4
  342.4 91.7 reduce-scatter.2
where the time goes:
time: 657 us; the launch traced here: 650 us
  blocking collectives  259 us (39%)
  waiting for transfers between devices  179 us (27%)
  local copies, waits for them, and re-layouts  116 us (18%)
  matrix products  35.9 us (5%)
  other arithmetic  30.4 us (5%)
  starting transfers between devices  15.3 us (2%)
  between operations  14.5 us (2%)
    reduce_scatter x1, waiting for transfers between devices, per_device(): lax.psum_scatter(arrange_sums(full_back, ctx_count, dp_count, exp_count,...  81.2 us
    reduce_scatter x1, waiting for transfers between devices, per_device(): lax.psum_scatter(arrange_sums(full_out, ctx_count, dp_count, exp_count, c...  60.3 us
    all_gather x2, blocking collectives, entering(): lax.all_gather(a.astype(kind), axis)  48.3 us
    psum x1, blocking collectives, per_device(): inner_sum = lax.psum(jnp.sum(hidden_f * scaled, axis=1), ('exp', 'dp'))  46.5 us
    psum x1, blocking collectives, per_device(): lax.psum((keys_first + keys_second).astype(jnp.bfloat16), ('exp', 'dp'))  45.7 us
    psum x1, blocking collectives, per_device(): grad_gain = lax.psum(gain_part, 'ctx')  39.5 us
    all_gather x1, waiting for transfers between devices, per_device(): all_rows = lax.all_gather(got_rows, ('ctx', 'dp'), axis=0, tiled=True)  35.8 us
    transpose x2, local copies, waits for them, and re-layouts, arrange_rows(): shaped.transpose(0, 2, 3, 1, 4)  26 us
  transfers between devices with their start and end apart: 6, of which 4 were waited for; matrix products, arithmetic and copies ran while one was open for 13% of the time, Pallas kernels for 0%

commit v1 on v0

--- a/solution.py
+++ b/solution.py
@@ -226,7 +226,11 @@
         out_grad.astype(jnp.float32) + inv_rms * scaled - hidden_f * inv_rms**3 * projection
     )
     gain_part = jnp.sum(grad_normed * hidden_f * inv_rms, axis=0)
-    grad_gain = lax.psum(gain_part, "ctx")
+    grad_gain = gain_part
+    for hop in (1, 2, 4, 8):
+        grad_gain = grad_gain + lax.ppermute(
+            grad_gain, "ctx", [(dev, dev ^ hop) for dev in range(16)]
+        )
     grad_mixer = grad_hidden.reshape(tokens, heads_here, head_size)
     vals_first, keys_first, queries_part, decay_first, carry_cot = output_pull(grad_mixer)
     grad_state = carried_in((decay_total, carry_cot), "ctx", combine_states, neutral)[1]

time: 657 us -> 632 us (0.962)
  blocking collectives: 259 us -> 220 us
  waiting for transfers between devices: 179 us -> 188 us
    psum x1 -> x0, blocking collectives: 39.5 us -> none  [per_device(): grad_gain = lax.psum(gain_part, 'ctx')]
    ppermute x0 -> x4, waiting for transfers between devices: none -> 8.6 us  [per_device(): lax.ppermute(grad_gain, 'ctx', [(dev, dev ^ hop) for dev in range(16)])]
  transfers between devices with their start and end apart: 6 -> 10, of which waited for: 4 -> 6; matrix products, arithmetic and copies ran while one was open for 13% -> 15% of each run, Pallas kernels for 0% -> 0%
where the time goes in v1:
time: 632 us; the launch traced here: 624 us
  blocking collectives  220 us (35%)
  waiting for transfers between devices  188 us (30%)
  local copies, waits for them, and re-layouts  116 us (18%)
  matrix products  35.9 us (6%)
  other arithmetic  31 us (5%)
  starting transfers between devices  18.4 us (3%)
  between operations  14.6 us (2%)
    reduce_scatter x1, waiting for transfers between devices, per_device(): lax.psum_scatter(arrange_sums(full_back, ctx_count, dp_count, exp_count,...  81.2 us
    reduce_scatter x1, waiting for transfers between devices, per_device(): lax.psum_scatter(arrange_sums(full_out, ctx_count, dp_count, exp_count, c...  60.4 us
    all_gather x2, blocking collectives, entering(): lax.all_gather(a.astype(kind), axis)  48.3 us
    psum x1, blocking collectives, per_device(): inner_sum = lax.psum(jnp.sum(hidden_f * scaled, axis=1), ('exp', 'dp'))  46.5 us
    psum x1, blocking collectives, per_device(): lax.psum((keys_first + keys_second).astype(jnp.bfloat16), ('exp', 'dp'))  46 us
    all_gather x1, waiting for transfers between devices, per_device(): all_rows = lax.all_gather(got_rows, ('ctx', 'dp'), axis=0, tiled=True)  36.2 us
    transpose x2, local copies, waits for them, and re-layouts, arrange_rows(): shaped.transpose(0, 2, 3, 1, 4)  26 us
    all_gather x1, blocking collectives, carried_in(): lax.all_gather(a.astype(kind), axis)  25 us
  transfers between devices with their start and end apart: 10, of which 6 were waited for; matrix products, arithmetic and copies ran while one was open for 15% of the time, Pallas kernels for 0%

profile of v1, /device:TPU:2, one launch (start us, length us, event | category | flops | bytes accessed | tf_op | source)
XLA Modules:
  0.0 624.2 jit_solution(6892878452611891266)
XLA Ops:
  7.3 0.9 copy.158
  11.6 13.2 %scatter_fusion = bf16[8,40,256]{2,1,0:T(8,128)(2,1)S(1)} fusion(bf16[8,40,256]{2,1,0:T(8,128)(2,1)S(1)} %broadcast_in_dim.73.clone.1, s32[256]{0:T(256)S(1)} %bitcast.193, bf16[256,256]{1,0:T(8,128)(2,1)S(1)} %fusion.19), kind=kCustom, calls=%fused_computation.2 | custom fusion | bytes 395264 | tf_op jit(solution)/shard_map/scatter | solution.py:188
  24.9 18.0 %all_to_all.66 = bf16[8,40,1,256]{3,1,2,0:T(8,128)(2,1)S(1)} all-to-all(bf16[8,40,1,256]{3,1,2,0:T(8,128)(2,1)S(1)} %bitcast.200), channel_id=1, replica_groups=mesh['ctx'=16,'exp'=8,'dp'=2] {'exp'}, dimensions={0} | all-to-all | bytes 327680 | tf_op jit(solution)/shard_map/all_to_all | solution.py:189
  44.6 20.7 %all-gather.4 = bf16[16,1,4]{2,1,0:T(2,128)(2,1)S(1)} all-gather(bf16[1,1,4]{2,1,0:T(2,128)(2,1)S(1)} %get-tuple-element.299), channel_id=1, replica_groups=mesh['ctx'=16,'exp'=8,'dp'=2] {'ctx'}, dimensions={0}, use_global_device_ids=true | all-gather | bytes 136 | tf_op jit(solution)/shard_map/all_gather | solution.py:13
  65.4 1.0 copy.152
  67.0 27.6 %all-gather = bf16[64,64,64]{2,1,0:T(8,128)(2,1)} all-gather(bf16[4,64,64]{2,1,0:T(8,128)(2,1)S(1)} %convolution_convert_fusion.4), channel_id=2, replica_groups=mesh['ctx'=16,'exp'=8,'dp'=2] {'ctx'}, dimensions={0}, use_global_device_ids=true | all-gather | bytes 557056 | tf_op jit(solution)/shard_map/all_gather | solution.py:13
  94.8 1.0 while.26
  94.9 0.9 convert_add_fusion.4
  96.7 23.5 %psum.35 = f32[128]{0:T(128)S(1)} all-reduce(f32[128]{0:T(128)S(1)} %get-tuple-element.291), channel_id=1, replica_groups=mesh['ctx'=16,'exp'=8,'dp'=2] {'exp','dp'}, use_global_device_ids=true, to_apply=%region_4.5 | all-reduce | flops 128 | bytes 1024 | tf_op jit(solution)/shard_map/psum | solution.py:153
  121.1 13.2 %scatter_fusion.1 = bf16[8,40,256]{2,1,0:T(8,128)(2,1)S(1)} fusion(bf16[8,40,256]{2,1,0:T(8,128)(2,1)S(1)} %broadcast_in_dim.73.clone, s32[256]{0:T(256)S(1)} %bitcast.194, bf16[256,256]{1,0:T(8,128)(2,1)S(1)} %reshape.273), kind=kCustom, calls=%fused_computation.3 | custom fusion | bytes 395264 | tf_op jit(solution)/shard_map/scatter | solution.py:162
  134.3 12.5 %all_to_all.67 = bf16[8,40,1,256]{3,1,2,0:T(8,128)(2,1)S(1)} all-to-all(bf16[8,40,1,256]{3,1,2,0:T(8,128)(2,1)S(1)} %bitcast.199), channel_id=1, replica_groups=mesh['ctx'=16,'exp'=8,'dp'=2] {'exp'}, dimensions={0} | all-to-all | bytes 327680 | tf_op jit(solution)/shard_map/all_to_all | solution.py:163
  147.8 13.0 %copy.164 = bf16[16,40,8,2,256]{4,3,2,1,0:T(2,128)(2,1)} copy(bf16[16,40,8,2,256]{4,2,1,3,0:T(8,128)(2,1)} %bitcast.203) | data formatting | bytes 10485760 | tf_op jit(solution)/shard_map/transpose | solution.py:105
  160.8 9.7 %reshape.236 = bf16[640,4096]{1,0:T(8,128)(2,1)} reshape(bf16[16,40,8,2,256]{4,3,2,1,0:T(2,128)(2,1)} %copy.164) | data formatting | bytes 10485760 | tf_op jit(solution)/shard_map/reshape | solution.py:105
  170.4 36.2 %all-gather.10.cloned.1.call-done = bf16[32,40,8,1,256]{4,2,3,1,0:T(8,128)(2,1)} async-done(((bf16[1,40,8,1,256]{4,2,3,1,0:T(8,128)(2,1)}), bf16[32,40,8,1,256]{4,2,3,1,0:T(8,128)(2,1)}) %all-gather.10.cloned.1.call-update) | async-done | bytes 5242896 | tf_op jit(solution)/shard_map/all_gather | solution.py:164
  206.6 13.0 %copy.167 = bf16[16,40,8,2,256]{4,3,2,1,0:T(2,128)(2,1)} copy(bf16[16,40,8,2,256]{4,2,1,3,0:T(8,128)(2,1)} %bitcast.204) | data formatting | bytes 10485760 | tf_op jit(solution)/shard_map/transpose | solution.py:105
  219.6 9.8 %reshape.240 = bf16[640,4096]{1,0:T(8,128)(2,1)} reshape(bf16[16,40,8,2,256]{4,3,2,1,0:T(2,128)(2,1)} %copy.167) | data formatting | bytes 10485760 | tf_op jit(solution)/shard_map/reshape | solution.py:105
  229.5 4.2 fusion.10
  234.2 1.5 fusion.5
  235.7 2.4 multiply_convert_fusion
  238.2 1.6 convert_bitcast_fusion
  239.7 2.2 copy.176
  241.9 4.6 copy.191
  246.8 1.3 copy-done.4
  248.2 1.6 fusion.3
  249.8 3.8 add_convert_fusion
  253.6 9.6 %convert_element_type.165 = bf16[16,40,8,2,256]{4,3,2,1,0:T(2,128)(2,1)} reshape(bf16[640,4096]{1,0:T(8,128)(2,1)} %add_convert_fusion) | data formatting | bytes 10485760 | tf_op jit(solution)/shard_map/convert_element_type | solution.py:201
  263.2 3.6 copy.168
  266.8 4.5 copy.189
  271.4 1.0 copy-done.10
  272.3 5.9 fusion.2
  278.2 60.4 %reduce-scatter.5.cloned.1.call-done = bf16[40,2048]{1,0:T(8,128)(2,1)} async-done(((bf16[1280,2048]{1,0:T(8,128)(2,1)}), bf16[40,2048]{1,0:T(8,128)(2,1)}) %reduce-scatter.5.cloned.1.call-update) | async-done | bytes 163856 | tf_op jit(solution)/shard_map/reduce_scatter | solution.py:173
  338.5 0.9 copy.192
  340.2 7.0 %all-to-all-start.3 = ((bf16[1,40,8,256]{3,1,0,2:T(8,128)(2,1)}), bf16[1,40,8,256]{3,1,0,2:T(8,128)(2,1)S(1)}, u32[]{:S(2)}, u32[]{:S(2)}) async-start(bf16[1,40,8,256]{3,1,0,2:T(8,128)(2,1)} %copy.177), calls=%async_computation.5 | async-start | bytes 327680 | tf_op jit(solution)/shard_map/all_to_all | solution.py:180
  347.2 5.7 fusion
  352.9 81.2 %reduce-scatter.3.cloned.1.call-done = bf16[40,2048]{1,0:T(8,128)(2,1)} async-done(((bf16[1280,2048]{1,0:T(8,128)(2,1)}), bf16[40,2048]{1,0:T(8,128)(2,1)}) %reduce-scatter.3.cloned.1.call-update) | async-done | bytes 163856 | tf_op jit(solution)/shard_map/reduce_scatter | solution.py:200
  434.1 0.9 copy.190
  435.8 7.3 %all-to-all-start.2 = ((bf16[1,40,8,256]{3,1,0,2:T(8,128)(2,1)}), bf16[1,40,8,256]{3,1,0,2:T(8,128)(2,1)S(1)}, u32[]{:S(2)}, u32[]{:S(2)}) async-start(bf16[1,40,8,256]{3,1,0,2:T(8,128)(2,1)} %copy.169), calls=%async_computation.3 | async-start | bytes 327680 | tf_op jit(solution)/shard_map/all_to_all | solution.py:207
  443.1 5.7 fusion.1
  448.8 1.7 gather_fusion.1
  450.7 1.7 all-to-all-done.2
  452.4 1.7 gather_fusion
  454.7 46.5 %all-reduce.1 = (f32[128]{0:T(128)S(1)}, f32[128,2]{1,0:T(8,128)S(1)}) all-reduce(f32[128]{0:T(128)S(1)} %get-tuple-element.264, f32[128,2]{1,0:T(8,128)S(1)} %reshape.247), channel_id=1, replica_groups=mesh['ctx'=16,'exp'=8,'dp'=2] {'exp','dp'}, use_global_device_ids=true, to_apply=%region_13.14 | all-reduce | flops 384 | bytes 3072 | tf_op jit(solution)/shard_map/psum | solution.py:223
  502.6 25.0 %all-gather.3 = bf16[64,64,64]{2,1,0:T(8,128)(2,1)} all-gather(bf16[4,64,64]{2,1,0:T(8,128)(2,1)S(1)} %convolution_convert_fusion.3), channel_id=5, replica_groups=mesh['ctx'=16,'exp'=8,'dp'=2] {'ctx'}, dimensions={0}, use_global_device_ids=true | all-gather | bytes 557056 | tf_op jit(solution)/shard_map/all_gather | solution.py:35
  527.6 22.9 %while.27 = (s32[]{:T(128)}, f32[4,64,64]{2,1,0:T(8,128)S(1)}, s32[]{:T(128)}, bf16[16,4]{1,0:T(8,128)(2,1)}, bf16[16,4,64,64]{3,2,1,0:T(8,128)(2,1)}, /*index=5*/s32[]{:T(128)}, s32[]{:T(128)}, s32[]{:T(128)}, s32[]{:T(128)}) while((s32[]{:T(128)}, f32[4,64,64]{2,1,0:T(8,128)S(1)}, s32[]{:T(128)}, bf16[16,4]{1,0:T(8,128)(2,1)}, ...), condition=%wide.region_15.16_spmd, body=%wide.region_14.15_spmd.sunk | while | flops 49162 | bytes 164035 | solution.py:52
  528.4 0.9 convert_add_fusion.5
  530.0 0.9 convert_add_fusion.5
  531.6 0.9 convert_add_fusion.5
  533.3 0.9 convert_add_fusion.5
  534.9 0.9 convert_add_fusion.5
  536.6 0.9 convert_add_fusion.5
  538.2 0.9 convert_add_fusion.5
  539.8 0.9 convert_add_fusion.5
  541.5 0.9 convert_add_fusion.5
  543.1 0.9 convert_add_fusion.5
  544.7 0.9 convert_add_fusion.5
  546.4 0.9 convert_add_fusion.5
  548.0 0.9 convert_add_fusion.5
  549.7 0.9 convert_add_fusion.5
  550.9 3.6 collective-permute-start
  556.6 5.0 collective-permute-done.1
  561.6 3.6 collective-permute-done.2
  565.2 46.0 %all-reduce.2 = (bf16[128,64]{0,1:T(8,128)(2,1)S(1)}, bf16[128,64]{0,1:T(8,128)(2,1)S(1)}) all-reduce(bf16[128,64]{0,1:T(8,128)(2,1)S(1)} %fusion.16, bf16[128,64]{0,1:T(8,128)(2,1)S(1)} %fusion.17), channel_id=1, replica_groups=mesh['ctx'=16,'exp'=8,'dp'=2] {'exp','dp'}, use_global_device_ids=true, to_apply=%region_17.18 | all-reduce | flops 16384 | bytes 65536 | tf_op jit(solution)/shard_map/psum | solution.py:240
  613.9 1.1 reduce_window_sum.47
  615.1 1.1 reduce_window_sum.48
  (150 shorter events, 29.2 us)
Async XLA Ops:
  7.2 222.2 %copy-start = (bf16[1,4096,256]{2,1,0:T(8,128)(2,1)S(1)}, bf16[1,4096,256]{2,1,0:T(8,128)(2,1)}, u32[]{:S(2)}) copy-start(bf16[1,4096,256]{2,1,0:T(8,128)(2,1)} %param.26) | copy-start | bytes 6291460
  7.2 59.6 %copy-start.13 = (bf16[128,64]{0,1:T(8,128)(2,1)S(1)}, bf16[128,64]{0,1:T(8,128)(2,1)}, u32[]{:S(2)}) copy-start(bf16[128,64]{0,1:T(8,128)(2,1)} %param.18) | copy-start | bytes 49156
  7.2 87.4 %copy-start.12 = (bf16[128,64]{0,1:T(8,128)(2,1)S(1)}, bf16[128,64]{0,1:T(8,128)(2,1)}, u32[]{:S(2)}) copy-start(bf16[128,64]{0,1:T(8,128)(2,1)} %param.19) | copy-start | bytes 49156
  7.2 89.4 %copy-start.16 = (bf16[128,256]{1,0:T(8,128)(2,1)S(1)}, bf16[128,256]{1,0:T(8,128)(2,1)}, u32[]{:S(2)}) copy-start(bf16[128,256]{1,0:T(8,128)(2,1)} %param.16) | copy-start | bytes 196612
  7.2 113.6 %copy-start.17 = (f32[256]{0:T(256)S(1)}, f32[256]{0:T(256)}, u32[]{:S(2)}) copy-start(f32[256]{0:T(256)} %param.23) | copy-start | bytes 3076
  7.2 140.5 %all-gather.8.cloned.1.call-start = ((), (), s32[]{:S(2)}) async-start(), calls=%async_computation.8 | async-start | bytes 5406720 | tf_op jit(solution)/shard_map/all_gather | solution.py:190
  43.6 163.0 %all-gather.10.cloned.1.call-start = ((), (), s32[]{:S(2)}) async-start(), calls=%async_computation.9 | async-start | bytes 5406720 | tf_op jit(solution)/shard_map/all_gather | solution.py:164
  66.4 67.9 %copy-start.19 = (f32[4,128]{1,0:T(4,128)}, f32[4,128]{1,0:T(4,128)S(1)}, u32[]{:S(2)}) copy-start(f32[4,128]{1,0:T(4,128)S(1)} %copy.150) | copy-start | bytes 6148
  94.8 39.5 %copy-start.14 = (f32[128,128]{1,0:T(8,128)}, f32[128,128]{1,0:T(8,128)S(1)}, u32[]{:S(2)}) copy-start(f32[128,128]{1,0:T(8,128)S(1)} %fusion.65) | copy-start | bytes 196612
  95.8 38.5 %copy-start.18 = (bf16[16,4]{1,0:T(8,128)(2,1)}, bf16[16,4]{1,0:T(8,128)(2,1)S(1)}, u32[]{:S(2)}) copy-start(bf16[16,4]{1,0:T(8,128)(2,1)S(1)} %get-tuple-element.441) | copy-start | bytes 388
  147.5 191.0 %reduce-scatter.5.cloned.1.call-start = ((), (), s32[]{:S(2)}) async-start(), calls=%async_computation.7 | async-start | bytes 5406720 | tf_op jit(solution)/shard_map/reduce_scatter | solution.py:173
  229.4 4.2 copy-start.2
  229.4 4.7 copy-start.3
  234.1 1.6 copy-start.5
  238.2 3.8 copy-start.9
  246.6 1.6 copy-start.4
  246.6 187.5 %reduce-scatter.3.cloned.1.call-start = ((), (), s32[]{:S(2)}) async-start(), calls=%async_computation.6 | async-start | bytes 5406720 | tf_op jit(solution)/shard_map/reduce_scatter | solution.py:200
  248.2 1.6 copy-start.6
  248.2 1.6 copy-start.7
  271.3 1.0 copy-start.10
  340.2 95.6 %all-to-all-start.3 = ((bf16[1,40,8,256]{3,1,0,2:T(8,128)(2,1)}), bf16[1,40,8,256]{3,1,0,2:T(8,128)(2,1)S(1)}, u32[]{:S(2)}, u32[]{:S(2)}) async-start(bf16[1,40,8,256]{3,1,0,2:T(8,128)(2,1)} %copy.177), calls=%async_computation.5 | async-start | bytes 327680 | tf_op jit(solution)/shard_map/all_to_all | solution.py:180
  347.2 95.8 %copy-start.8 = (bf16[640,256]{1,0:T(8,128)(2,1)S(1)}, bf16[640,256]{1,0:T(8,128)(2,1)}, u32[]{:S(2)}) copy-start(bf16[640,256]{1,0:T(8,128)(2,1)} %get-tuple-element.297) | copy-start | bytes 983044
  435.8 16.6 %all-to-all-start.2 = ((bf16[1,40,8,256]{3,1,0,2:T(8,128)(2,1)}), bf16[1,40,8,256]{3,1,0,2:T(8,128)(2,1)S(1)}, u32[]{:S(2)}, u32[]{:S(2)}) async-start(bf16[1,40,8,256]{3,1,0,2:T(8,128)(2,1)} %copy.169), calls=%async_computation.3 | async-start | bytes 327680 | tf_op jit(solution)/shard_map/all_to_all | solution.py:207
  443.0 58.1 %copy-start.11 = (bf16[128,256]{1,0:T(8,128)(2,1)S(1)}, bf16[128,256]{1,0:T(8,128)(2,1)}, u32[]{:S(2)}) copy-start(bf16[128,256]{1,0:T(8,128)(2,1)} %param.27) | copy-start | bytes 196612
  443.1 58.1 %copy-start.21 = (f32[128]{0:T(128)S(1)}, f32[128]{0:T(128)}, u32[]{:S(2)}) copy-start(f32[128]{0:T(128)} %get-tuple-element.300) | copy-start | bytes 1540
  448.8 105.7 %copy-start.15 = (f32[128,128]{1,0:T(8,128)S(1)}, f32[128,128]{1,0:T(8,128)}, u32[]{:S(2)}) copy-start(f32[128,128]{1,0:T(8,128)} %copy-done.14) | copy-start | bytes 196612
  448.8 105.7 %copy-start.20 = (f32[4,128]{1,0:T(4,128)S(1)}, f32[4,128]{1,0:T(4,128)}, u32[]{:S(2)}) copy-start(f32[4,128]{1,0:T(4,128)} %copy-done.19) | copy-start | bytes 6148
  452.4 165.0 %copy-start.1 = (bf16[1,4096,256]{2,1,0:T(8,128)(2,1)S(1)}, bf16[1,4096,256]{2,1,0:T(8,128)(2,1)}, u32[]{:S(2)}) copy-start(bf16[1,4096,256]{2,1,0:T(8,128)(2,1)} %param.26) | copy-start | bytes 6291460
  550.9 5.5 collective-permute-start
  556.5 5.2 collective-permute-start.1
  561.6 3.6 collective-permute-start.2
  565.2 51.6 %collective-permute-start.3 = (f32[256]{0:T(256)S(1)}, f32[256]{0:T(256)S(1)}, u32[]{:S(2)}, u32[]{:S(2)}) collective-permute-start(f32[256]{0:T(256)S(1)} %add.141), channel_id=1, source_target_pairs={{0,128},{16,144},{32,160},{48,176},{64,192},{80,208},{96,224},{112... | collective-permute-start | bytes 3080 | tf_op jit(solution)/shard_map/ppermute | solution.py:231
Sparse Core Ops, SparseCore 0:
  43.7 49.1 all-gather.7
  147.6 58.9 all-gather.9
  246.7 91.7 reduce-scatter.4
  342.4 91.6 reduce-scatter.2
